TPU v7x, 32 devices: a whole 2x2x4 slice. The times are simulated.
32 devices in a mesh: freq: 4 (over x, core), tile: 8 (over z, y).
Axes of the slice: x: 2, y: 2, z: 4, core: 2. Of those that a mesh axis runs over, the one named last changes fastest.
Arguments:
- plus_time: bfloat16 [128, 128, 12288], P('freq', None, 'tile'), may hold values from -6 to 6
- minus_time: bfloat16 [128, 128, 12288], P('freq', None, 'tile'), may hold values from -6 to 6
- gate_starts: int32 [128, 48], P('freq', 'tile'), may hold values from 0 to 64
- tile_ranks: int32 [4, 48, 48], P('freq', None, 'tile'), may hold values from 1 to 64, as said below
- u_factors: bfloat16 [4, 48, 48, 2, 64, 256], P('freq', 'tile'), may hold values from -0.109375 to 0.109375
- v_factors: bfloat16 [4, 48, 48, 2, 64, 256], P('freq', None, 'tile'), may hold values from -0.375 to 0.375
Outputs:
- minus_new: bfloat16 [4, 2, 128, 12288], P('freq', None, None, 'tile')
- plus_new: bfloat16 [4, 2, 128, 12288], P('freq', None, None, 'tile')
- cross_gram: float32 [4, 2, 128, 128], P('freq', None, 'tile')
- normal_gram: float32 [4, 2, 128, 128], P('freq', None, 'tile')
Inputs may be any that keep to these rules, and one draw needn't show every extreme that they name: `tile_ranks`: tiles with |i - j| <= 1 have rank 64; every other tile has rank at most 32, and some tile of every draw has exactly 32.
All inputs are finite; a program needn't handle non-finite values.
Results may differ from a plain program's by a relative error of at most 0.014.
Values may be sent and summed in bfloat16 or wider, within the bound.
A program may use at most 192 MiB of HBM per device.

v0:
```python
import functools
import math

import jax
import jax.numpy as jnp
from jax import lax
from jax.experimental import pallas as pl
from jax.experimental.pallas import tpu as pltpu
from jax.sharding import PartitionSpec as P

GATE = 64
MESH = pl.DeviceIdType.MESH
NT_DIMS = (((1,), (1,)), ((), ()))
TN_DIMS = (((0,), (0,)), ((), ()))


def make_table(freq_count, sample_count):
    freq_ids = lax.broadcasted_iota(jnp.int32, (freq_count, sample_count), 0)
    sample_ids = lax.broadcasted_iota(jnp.int32, (freq_count, sample_count), 1)
    phase_ids = freq_ids * sample_ids % sample_count
    angles = phase_ids.astype(jnp.float32) * (2.0 * math.pi / sample_count)
    amplitude = 1.0 / math.sqrt(GATE)
    return jnp.stack([jnp.cos(angles) * amplitude, -jnp.sin(angles) * amplitude]).astype(
        jnp.bfloat16
    )


def gate_table(freq_total, samples, block):
    table = make_table(freq_total, samples).transpose(1, 0, 2).astype(jnp.float32)
    table = jnp.broadcast_to(table[:, :, None, None], (freq_total, 2, block, 2, samples))
    return table.reshape(freq_total * 2 * block, 2 * samples)


def partner(me, step):
    other, bit = me, 1
    while bit <= step:
        if step & bit:
            other = other + bit - 2 * bit * ((me // bit) % 2)
        bit *= 2
    return other


def swapped(block, count, axis):
    parts = [lax.slice_in_dim(block, n * count, (n + 1) * count, axis=axis) for n in range(4)]
    return jnp.concatenate([-parts[2], parts[3], parts[0], -parts[1]], axis=axis)


def operator_kernel(
    n, nf, starts, ranks, table, plus_hbm, minus_hbm, u_hbm, v_hbm, minus, plus, cross, normal,
    spec, traces, sem_t, xall, v_s, u_s, vb, ub, send, recv, cband, bin_, acc, gsum, gsend, grecv,
    sem_v, sem_u, sem_vb, sem_ub, fsend, frecv, csend, crecv, bsend, brecv, gs_sem, gr_sem,
):
    me = lax.axis_index("tile")
    mf = lax.axis_index("freq")
    tiles, half, width = v_s.shape[0], v_s.shape[3], v_s.shape[4]
    sl = spec.shape[3]
    count = sl * nf
    lanes = 4 * count
    base = me * tiles
    total_tiles = n * tiles
    first = 1 - (me + n - 1) // n
    last = (me + 1) // n
    inner = ((me + n // 4) // (n // 2)) % 2

    def load_v(j):
        return pltpu.make_async_copy(
            v_hbm.at[0, :, j, :, pl.ds(0, half), :], v_s.at[j], sem_v.at[j]
        )

    def load_u(m):
        src = partner(me, m)
        return pltpu.make_async_copy(
            u_hbm.at[0, :, pl.ds(src * tiles, tiles), :, pl.ds(0, half), :], u_s.at[m], sem_u.at[m]
        )

    def load_band(o, j, right):
        row, col = base + j + o - 1, base + j - o + 1
        if j + o - 1 < 0:
            row = row + first
        if j + o - 1 >= tiles:
            row = row - last
        if j - o + 1 < 0:
            col = col + first
        if j - o + 1 >= tiles:
            col = col - last
        if right:
            return pltpu.make_async_copy(
                v_hbm.at[0, row, j, :, pl.ds(half, half), :], vb.at[o, j], sem_vb.at[o, j]
            )
        return pltpu.make_async_copy(
            u_hbm.at[0, j, col, :, pl.ds(half, half), :], ub.at[o, j], sem_ub.at[o, j]
        )

    def columns(j):
        return pl.ds(pl.multiple_of(j * width, width), width)

    def freq_copy(g, j):
        peer = partner(mf, g)
        return pltpu.make_async_remote_copy(
            src_ref=spec.at[peer, :, :, :, columns(j)],
            dst_ref=xall.at[:, :, pl.ds(pl.multiple_of(mf * sl, sl), sl), columns(j)],
            send_sem=fsend.at[g, j],
            recv_sem=frecv.at[g, j],
            device_id={"freq": peer},
            device_id_type=MESH,
        )

    def coeff_copy(m, j):
        return pltpu.make_async_remote_copy(
            src_ref=send.at[j, m],
            dst_ref=recv.at[j, m],
            send_sem=csend.at[m, j],
            recv_sem=crecv.at[m, j],
            device_id={"tile": partner(me, m)},
            device_id_type=MESH,
        )

    def band_copy(side):
        source = cband.at[2, tiles + 1] if side == 0 else cband.at[0, 0]
        target = lax.rem(me + 1, n) if side == 0 else lax.rem(me + n - 1, n)
        return pltpu.make_async_remote_copy(
            src_ref=source,
            dst_ref=bin_.at[side],
            send_sem=bsend.at[side],
            recv_sem=brecv.at[side],
            device_id={"tile": target},
            device_id_type=MESH,
        )

    def gram_copy(m):
        other = partner(me, m)
        return pltpu.make_async_remote_copy(
            src_ref=gsend.at[other],
            dst_ref=grecv.at[m],
            send_sem=gs_sem.at[m],
            recv_sem=gr_sem.at[m],
            device_id={"tile": other},
            device_id_type=MESH,
        )

    def load_traces(q, j):
        source = minus_hbm if q else plus_hbm
        return pltpu.make_async_copy(
            source.at[:, :, columns(j)], traces.at[j % 2, q], sem_t.at[q, j]
        )

    for j in range(min(2, tiles)):
        load_traces(0, j).start()
        load_traces(1, j).start()
    for j in range(tiles):
        load_v(j).start()
        for o in range(3):
            load_band(o, j, True).start()
            load_band(o, j, False).start()
    for m in range(n):
        load_u(m).start()

    barrier = pltpu.get_barrier_semaphore()
    for m in range(1, n):
        pl.semaphore_signal(
            barrier, inc=1, device_id={"tile": partner(me, m)}, device_id_type=MESH
        )
    for g in range(1, nf):
        pl.semaphore_signal(
            barrier, inc=1, device_id={"freq": partner(mf, g)}, device_id_type=MESH
        )
    pl.semaphore_wait(barrier, n + nf - 2)

    samples = traces.shape[3]
    rows = table.shape[0]
    sources = rows // (2 * nf)
    shape = (2 * nf, sources, 2 * samples)
    row_source = lax.broadcasted_iota(jnp.int32, shape, 1).reshape(rows, 2 * samples)
    column = lax.broadcasted_iota(jnp.int32, (rows, 2 * samples), 1)
    second = column >= samples
    sample = jnp.where(second, column - samples, column)
    row_source = row_source - second.astype(jnp.int32)

    def spectra(j):
        load_traces(0, j).wait()
        load_traces(1, j).wait()
        for block in range(sl // sources):
            totals = [jnp.zeros((rows, width), jnp.float32) for _ in range(2)]
            for pair in range(sources // 2):
                first_id = block * sources + 2 * pair
                start = jnp.where(second, starts[first_id + 1, j], starts[first_id, j])
                inside = (sample >= start) & (sample < start + GATE) & (row_source == 2 * pair)
                gated = jnp.where(inside, table[...], 0.0).astype(jnp.bfloat16)
                for q in range(2):
                    values = traces[j % 2, q, first_id : first_id + 2]
                    totals[q] += jnp.dot(
                        gated,
                        values.reshape(2 * samples, width),
                        preferred_element_type=jnp.float32,
                    )
            part = slice(block * sources, (block + 1) * sources)
            for q in range(2):
                spec[:, :, q, part, columns(j)] = (
                    totals[q].reshape(nf, 2, sources, width).astype(jnp.bfloat16)
                )
        for g in range(1, nf):
            freq_copy(g, j).start()
        xall[:, :, pl.ds(pl.multiple_of(mf * sl, sl), sl), columns(j)] = spec[mf, :, :, :, columns(j)]

        @pl.when(j + 2 < tiles)
        def _():
            load_traces(0, j + 2).start()
            load_traces(1, j + 2).start()

    acc[...] = jnp.zeros_like(acc)
    for j in range(tiles):
        for o in range(3):
            load_band(o, j, True).wait()

    rank_id = lax.broadcasted_iota(jnp.int32, (half, lanes), 0)

    def product(a_real, a_imag, b_one, b_two):
        return lax.dot_general(
            a_real, b_one, NT_DIMS, preferred_element_type=jnp.float32
        ) + lax.dot_general(a_imag, b_two, NT_DIMS, preferred_element_type=jnp.float32)

    def coefficients(j):
        for g in range(1, nf):
            freq_copy(g, j).wait_recv()
        load_v(j).wait()
        b_one = xall[:, :, :, columns(j)].reshape(lanes, width)
        b_two = swapped(b_one, count, 0)
        for m in list(range(1, n)) + [0]:
            row = partner(me, m) * tiles
            c = product(
                v_s[j, pl.ds(row, tiles), 0].reshape(tiles * half, width),
                v_s[j, pl.ds(row, tiles), 1].reshape(tiles * half, width),
                b_one,
                b_two,
            )
            target = send if m else recv
            for i in range(tiles):
                kept = jnp.where(
                    rank_id < ranks[0, row + i, j], c[i * half : (i + 1) * half], 0.0
                )
                target[j, m, i] = kept.astype(jnp.bfloat16)
            if 0 < m < n // 2:
                coeff_copy(m, j).start()
            elif m:

                @pl.when(inner == 1)
                def _():
                    coeff_copy(m, j).start()

        c = product(
            vb[:, j, 0].reshape(3 * half, width), vb[:, j, 1].reshape(3 * half, width), b_one, b_two
        ).astype(jnp.bfloat16)
        for o in range(3):
            cband[o, j + o] = c[o * half : (o + 1) * half]

    def advance(step, _):
        @pl.when(step < tiles)
        def _():
            spectra(step)

        @pl.when(step > 0)
        def _():
            coefficients(step - 1)

        return 0

    lax.fori_loop(0, tiles + 1, advance, 0)

    @pl.when(inner == 0)
    def _():
        for j in range(tiles):
            for m in range(n // 2, n):
                coeff_copy(m, j).start()

    band_copy(0).start()
    band_copy(1).start()
    for m in range(n):
        load_u(m).wait()
    for j in range(tiles):
        for o in range(3):
            load_band(o, j, False).wait()

    def add(i, c, u_real, u_imag):
        acc[i] += lax.dot_general(
            c, u_real, TN_DIMS, preferred_element_type=jnp.float32
        ) + lax.dot_general(
            swapped(c, count, 1), u_imag, TN_DIMS, preferred_element_type=jnp.float32
        )

    def responses(j, _):
        for m in range(1, n):
            coeff_copy(m, j).wait_recv()

        def one_row(i, _):
            add(
                i,
                recv[j, :, i].reshape(n * half, lanes),
                u_s[:, i, j, 0].reshape(n * half, width),
                u_s[:, i, j, 1].reshape(n * half, width),
            )
            return 0

        return lax.fori_loop(0, tiles, one_row, 0)

    lax.fori_loop(0, tiles - 1, responses, 0)
    band_copy(0).wait_recv()
    band_copy(1).wait_recv()
    zero = jnp.zeros((half, lanes), jnp.bfloat16)
    from_before = jnp.where(first == 0, bin_[0], zero)
    from_after = jnp.where(last == 0, bin_[1], zero)
    for i in range(tiles):
        c = [cband[o, i + 1] for o in range(3)]
        if i == 0:
            c[2] = from_before
        if i == tiles - 1:
            c[0] = from_after
        add(
            i,
            jnp.concatenate(c, axis=0),
            ub[:, i, 0].reshape(3 * half, width),
            ub[:, i, 1].reshape(3 * half, width),
        )
    responses(tiles - 1, 0)

    gsum[...] = jnp.zeros_like(gsum)

    def finish(i, _):
        rounded = acc[i].astype(jnp.bfloat16)
        parts = [rounded[p * count : (p + 1) * count] for p in range(4)]
        for c in range(2):
            minus[0, c, :, columns(i)] = parts[2 * c]
            plus[0, c, :, columns(i)] = parts[2 * c + 1]
        gsum[...] += lax.dot_general(
            rounded,
            jnp.concatenate([parts[1], parts[3]], axis=0),
            NT_DIMS,
            preferred_element_type=jnp.float32,
        )
        return 0

    lax.fori_loop(0, tiles, finish, 0)
    receivers = total_tiles * width
    share = count // n
    for q, scale in enumerate((1.0 / math.sqrt(receivers), 1.0 / receivers)):
        top = slice(q * count, (q + 1) * count)
        low = slice((2 + q) * count, (3 + q) * count)
        real = (gsum[top, :count] + gsum[low, count:]) * scale
        imag = (gsum[low, :count] - gsum[top, count:]) * scale
        for d in range(n):
            gsend[d, q, 0] = real[d * share : (d + 1) * share]
            gsend[d, q, 1] = imag[d * share : (d + 1) * share]
    for m in range(1, n):
        gram_copy(m).start()
    total = gsend[me]
    for m in range(1, n):
        gram_copy(m).wait_recv()
        total = total + grecv[m]
    cross[0] = total[0]
    normal[0] = total[1]

    for j in range(tiles):
        for g in range(1, nf):
            freq_copy(g, j).wait_send()
        for m in range(1, n):
            coeff_copy(m, j).wait_send()
    band_copy(0).wait_send()
    band_copy(1).wait_send()
    for m in range(1, n):
        gram_copy(m).wait_send()


def on_device(n, nf, plus_time, minus_time, gate_starts, tile_ranks, u_factors, v_factors):
    freq_total = u_factors.shape[0] * nf
    tiles = v_factors.shape[2]
    half = v_factors.shape[4] // 2
    width = v_factors.shape[5]
    sl, samples, receivers = plus_time.shape
    table = gate_table(freq_total, samples, math.gcd(16, sl))
    count = sl * nf
    lanes = 4 * count
    share = count // n
    bf16, f32 = jnp.bfloat16, jnp.float32
    vmem = pl.BlockSpec(memory_space=pltpu.VMEM)
    dma = pltpu.SemaphoreType.DMA
    return pl.pallas_call(
        functools.partial(operator_kernel, n, nf),
        out_shape=(
            jax.ShapeDtypeStruct((1, 2, count, receivers), bf16),
            jax.ShapeDtypeStruct((1, 2, count, receivers), bf16),
            jax.ShapeDtypeStruct((1, 2, share, count), f32),
            jax.ShapeDtypeStruct((1, 2, share, count), f32),
        ),
        in_specs=[
            pl.BlockSpec(memory_space=pltpu.SMEM),
            pl.BlockSpec(memory_space=pltpu.SMEM),
            vmem,
            pl.BlockSpec(memory_space=pl.ANY),
            pl.BlockSpec(memory_space=pl.ANY),
            pl.BlockSpec(memory_space=pl.ANY),
            pl.BlockSpec(memory_space=pl.ANY),
        ],
        out_specs=(vmem, vmem, vmem, vmem),
        scratch_shapes=[
            pltpu.VMEM((freq_total, 2, 2, sl, receivers), bf16),
            pltpu.VMEM((2, 2, sl, samples, width), bf16),
            dma((2, tiles)),
            pltpu.VMEM((2, 2, count, receivers), bf16),
            pltpu.VMEM((tiles, n * tiles, 2, half, width), bf16),
            pltpu.VMEM((n, tiles, tiles, 2, half, width), bf16),
            pltpu.VMEM((3, tiles, 2, half, width), bf16),
            pltpu.VMEM((3, tiles, 2, half, width), bf16),
            pltpu.VMEM((tiles, n, tiles, half, lanes), bf16),
            pltpu.VMEM((tiles, n, tiles, half, lanes), bf16),
            pltpu.VMEM((3, tiles + 2, half, lanes), bf16),
            pltpu.VMEM((2, half, lanes), bf16),
            pltpu.VMEM((tiles, lanes, width), f32),
            pltpu.VMEM((lanes, 2 * count), f32),
            pltpu.VMEM((n, 2, 2, share, count), f32),
            pltpu.VMEM((n, 2, 2, share, count), f32),
            dma((tiles,)),
            dma((n,)),
            dma((3, tiles)),
            dma((3, tiles)),
            dma((nf, tiles)),
            dma((nf, tiles)),
            dma((n, tiles)),
            dma((n, tiles)),
            dma((2,)),
            dma((2,)),
            dma((n,)),
            dma((n,)),
        ],
        compiler_params=pltpu.CompilerParams(
            collective_id=0, has_side_effects=True, vmem_limit_bytes=63 << 20
        ),
        name="reflection_operator",
    )(
        gate_starts, tile_ranks, table, plus_time, minus_time, u_factors, v_factors
    )


def solution(mesh):
    placed = (
        P("freq", None, "tile"),
        P("freq", None, "tile"),
        P("freq", "tile"),
        P("freq", None, "tile"),
        P("freq", "tile", None, None, None, None),
        P("freq", None, "tile", None, None, None),
    )
    return jax.shard_map(
        functools.partial(on_device, mesh.shape["tile"], mesh.shape["freq"]),
        mesh=mesh,
        in_specs=placed,
        out_specs=(
            P("freq", None, None, "tile"),
            P("freq", None, None, "tile"),
            P("freq", None, "tile", None),
            P("freq", None, "tile", None),
        ),
        check_vma=False,
    )
```

profile of v0, /device:TPU:0, one launch (start us, length us, event | category | flops | bytes accessed | tf_op | source)
XLA Modules:
  0.0 252.2 jit_solution(11657819628049258793)
XLA Ops:
  0.6 0.1 multiply_convert_fusion
  0.7 1.4 copy.13.starts
  2.1 1.4 copy.14.ranks
  3.5 0.7 copy.17
  4.2 241.3 %reflection_operator.1 = (bf16[1,2,128,1536]{3,2,1,0:T(8,128)(2,1)}, bf16[1,2,128,1536]{3,2,1,0:T(8,128)(2,1)}, f32[1,2,16,128]{3,2,1,0:T(8,128)}, f32[1,2,16,128]{3,2,1,0:T(8,128)}) custom-call(s32[32,6]{1,0:T(8,128)} %copy.13.starts, s32[1,48,6]{2,1,0:T(8,128)} %copy.14.ranks, f32[128,256]{1,0:T(8,128)} %bitcast.7, bf16[32,128,1536]{2,1,0:T(8,128)(2,1)} %plus_hbm.1, ...), custom_call_target="tpu_custom_call" | custom-call | tf_op jit(solution)/shard_map/reflection_operator/pallas_call | solution.py:385
  245.4 2.1 copy.22
  247.5 2.1 copy.23
  249.6 1.3 copy.24
  250.9 1.3 copy.25
  (3 shorter events, 0.1 us)
where the time goes:
time: 253 us; the launch traced here: 252 us
  Pallas kernels  241 us (95%)
  local copies, waits for them, and re-layouts  10.2 us (4%)
    pallas_call x1, Pallas kernels, on_device(): pl.pallas_call(functools.partial(operator_kernel, n, nf), out_shape=(jax....  241 us
    unnamed x7, local copies, waits for them, and re-layouts  10.2 us

commit v1 on v0

v1 whole, which is shorter than its diff:
```python
import functools
import math

import jax
import jax.numpy as jnp
from jax import lax
from jax.experimental import pallas as pl
from jax.experimental.pallas import tpu as pltpu
from jax.sharding import PartitionSpec as P

GATE = 64
MESH = pl.DeviceIdType.MESH
NT_DIMS = (((1,), (1,)), ((), ()))
TN_DIMS = (((0,), (0,)), ((), ()))


def make_table(freq_count, sample_count):
    freq_ids = lax.broadcasted_iota(jnp.int32, (freq_count, sample_count), 0)
    sample_ids = lax.broadcasted_iota(jnp.int32, (freq_count, sample_count), 1)
    phase_ids = freq_ids * sample_ids % sample_count
    angles = phase_ids.astype(jnp.float32) * (2.0 * math.pi / sample_count)
    amplitude = 1.0 / math.sqrt(GATE)
    return jnp.stack([jnp.cos(angles) * amplitude, -jnp.sin(angles) * amplitude]).astype(
        jnp.bfloat16
    )


def gate_table(freq_total, samples):
    table = make_table(freq_total, samples).transpose(1, 0, 2).astype(jnp.float32)
    table = table.reshape(freq_total * 2, samples)
    return jnp.concatenate([table, table], axis=1)


def partner(me, step, n):
    other, bit = 0, 1
    while bit < n:
        other = other + bit * ((me // bit + step // bit) % 2)
        bit *= 2
    return other


def swapped(block, count, axis):
    parts = [lax.slice_in_dim(block, n * count, (n + 1) * count, axis=axis) for n in range(4)]
    return jnp.concatenate([-parts[2], parts[3], parts[0], -parts[1]], axis=axis)


def operator_kernel(
    n, nf, starts_hbm, ranks_hbm, table_hbm, plus_hbm, minus_hbm, u_hbm, v_hbm,
    minus, plus, cross, normal,
    starts, ranks, small, table, spec, traces, xall, v_s, u_s, vb, ub, send, recv, cband, bin_,
    acc, gsum, gsend, grecv,
    sem_s, sem_t, sem_v, sem_u, sem_vb, sem_ub, fsend, frecv, csend, crecv, rsend, rrecv,
    bsend, brecv, gs_sem, gr_sem,
):
    me = lax.axis_index("tile")
    mf = lax.axis_index("freq")
    tiles, half, width = v_s.shape[0], v_s.shape[3], v_s.shape[4]
    sl = spec.shape[3]
    count = sl * nf
    lanes = 4 * count
    base = me * tiles
    total_tiles = n * tiles
    samples = traces.shape[3]
    rows = table.shape[0]
    sources = rows // (2 * nf)
    blocks = sl // sources
    first = 1 - (me + n - 1) // n
    last = (me + 1) // n
    inner = ((me + n // 4) // (n // 2)) % 2

    def load_v(j):
        return pltpu.make_async_copy(
            v_hbm.at[0, :, j, :, pl.ds(0, half), :], v_s.at[j], sem_v.at[j]
        )

    def load_u(m):
        src = partner(me, m, n)
        return pltpu.make_async_copy(
            u_hbm.at[0, :, pl.ds(src * tiles, tiles), :, pl.ds(0, half), :],
            u_s.at[:, pl.ds(m * tiles, tiles)],
            sem_u.at[m],
        )

    def load_band(o, j, right):
        row, col = base + j + o - 1, base + j - o + 1
        if j + o - 1 < 0:
            row = row + first
        if j + o - 1 >= tiles:
            row = row - last
        if j - o + 1 < 0:
            col = col + first
        if j - o + 1 >= tiles:
            col = col - last
        if right:
            return pltpu.make_async_copy(
                v_hbm.at[0, row, j, :, pl.ds(half, half), :], vb.at[o, j], sem_vb.at[o, j]
            )
        return pltpu.make_async_copy(
            u_hbm.at[0, j, col, :, pl.ds(half, half), :], ub.at[o, j], sem_ub.at[o, j]
        )

    def columns(j):
        return pl.ds(pl.multiple_of(j * width, width), width)

    def freq_copy(g, j, block):
        peer = partner(mf, g, nf)
        part = pl.ds(block * sources, sources)
        place = pl.ds(pl.multiple_of(mf * sl + block * sources, sources), sources)
        return pltpu.make_async_remote_copy(
            src_ref=spec.at[peer, :, :, part, columns(j)],
            dst_ref=xall.at[:, :, place, columns(j)],
            send_sem=fsend.at[g, j, block],
            recv_sem=frecv.at[g, j, block],
            device_id={"freq": peer},
            device_id_type=MESH,
        )

    def slots(m, j, size):
        return pl.ds((m * tiles + j) * half, size * half)

    def first_copy(m):
        return pltpu.make_async_remote_copy(
            src_ref=send.at[m, :, pl.ds(0, half)],
            dst_ref=recv.at[:, slots(m, 0, 1)],
            send_sem=csend.at[m],
            recv_sem=crecv.at[m],
            device_id={"tile": partner(me, m, n)},
            device_id_type=MESH,
        )

    def row_copy(m, i):
        return pltpu.make_async_remote_copy(
            src_ref=send.at[m, i, pl.ds(half, (tiles - 1) * half)],
            dst_ref=recv.at[i, slots(m, 1, tiles - 1)],
            send_sem=rsend.at[m, i],
            recv_sem=rrecv.at[m, i],
            device_id={"tile": partner(me, m, n)},
            device_id_type=MESH,
        )

    def band_copy(side):
        source = cband.at[2, tiles + 1] if side == 0 else cband.at[0, 0]
        target = lax.rem(me + 1, n) if side == 0 else lax.rem(me + n - 1, n)
        return pltpu.make_async_remote_copy(
            src_ref=source,
            dst_ref=bin_.at[side],
            send_sem=bsend.at[side],
            recv_sem=brecv.at[side],
            device_id={"tile": target},
            device_id_type=MESH,
        )

    def gram_copy(m):
        other = partner(me, m, n)
        return pltpu.make_async_remote_copy(
            src_ref=gsend.at[other],
            dst_ref=grecv.at[m],
            send_sem=gs_sem.at[m],
            recv_sem=gr_sem.at[m],
            device_id={"tile": other},
            device_id_type=MESH,
        )

    def load_traces(q, j, block):
        source = minus_hbm if q else plus_hbm
        part = pl.ds(block * sources, sources)
        return pltpu.make_async_copy(
            source.at[part, :, columns(j)], traces.at[j % 2, q, part], sem_t.at[q, j, block]
        )

    barrier = pltpu.get_barrier_semaphore()
    for m in range(1, n):
        pl.semaphore_signal(
            barrier, inc=1, device_id={"tile": partner(me, m, n)}, device_id_type=MESH
        )
    for g in range(1, nf):
        pl.semaphore_signal(
            barrier, inc=1, device_id={"freq": partner(mf, g, nf)}, device_id_type=MESH
        )

    small_copies = [
        pltpu.make_async_copy(table_hbm, small, sem_s.at[0]),
        pltpu.make_async_copy(starts_hbm, starts, sem_s.at[1]),
        pltpu.make_async_copy(ranks_hbm, ranks, sem_s.at[2]),
    ]
    for copy in small_copies:
        copy.start()
    for j in range(min(2, tiles)):
        for block in range(blocks):
            for q in range(2):
                load_traces(q, j, block).start()
        load_v(j).start()
        if j == 0:
            for o in range(3):
                for jj in range(tiles):
                    load_band(o, jj, True).start()

    shape = (2 * nf, sources, 2 * samples)
    row_source = lax.broadcasted_iota(jnp.int32, shape, 1).reshape(rows, 2 * samples)
    column = lax.broadcasted_iota(jnp.int32, (rows, 2 * samples), 1)
    second = column >= samples
    sample = jnp.where(second, column - samples, column)
    row_source = row_source - second.astype(jnp.int32)
    for copy in small_copies:
        copy.wait()
    table[...] = jnp.broadcast_to(small[...][:, None, :], shape).reshape(rows, 2 * samples)

    def own_rows(block):
        return pl.ds(pl.multiple_of(mf * sl + block * sources, sources), sources)

    def spectra(j, block):
        for q in range(2):
            load_traces(q, j, block).wait()
        totals = [jnp.zeros((rows, width), jnp.float32) for _ in range(2)]
        for pair in range(sources // 2):
            first_id = block * sources + 2 * pair
            start = jnp.where(second, starts[j, first_id + 1], starts[j, first_id])
            inside = (sample >= start) & (sample < start + GATE) & (row_source == 2 * pair)
            gated = jnp.where(inside, table[...], 0.0).astype(jnp.bfloat16)
            for q in range(2):
                values = traces[j % 2, q, first_id : first_id + 2]
                totals[q] += jnp.dot(
                    gated,
                    values.reshape(2 * samples, width),
                    preferred_element_type=jnp.float32,
                )
        part = slice(block * sources, (block + 1) * sources)
        for q in range(2):
            spec[:, :, q, part, columns(j)] = (
                totals[q].reshape(nf, 2, sources, width).astype(jnp.bfloat16)
            )

    def share_spectra(j, block):
        for g in range(nf - 1, 0, -1):
            freq_copy(g, j, block).start()
        part = slice(block * sources, (block + 1) * sources)
        xall[:, :, own_rows(block), columns(j)] = spec[mf, :, :, part, columns(j)]

    rank_id = lax.broadcasted_iota(jnp.int32, (half, lanes), 0)

    def product(a_real, a_imag, b_one, b_two):
        return lax.dot_general(
            a_real, b_one, NT_DIMS, preferred_element_type=jnp.float32
        ) + lax.dot_general(a_imag, b_two, NT_DIMS, preferred_element_type=jnp.float32)

    def coefficients(j, leading):
        for block in range(blocks):
            for g in range(1, nf):
                freq_copy(g, j, block).wait_recv()
        load_v(j).wait()
        b_one = xall[:, :, :, columns(j)].reshape(lanes, width)
        b_two = swapped(b_one, count, 0)

        def tile_block(m, own):
            row = partner(me, m, n) * tiles
            c = product(
                v_s[j, pl.ds(row, tiles), 0].reshape(tiles * half, width),
                v_s[j, pl.ds(row, tiles), 1].reshape(tiles * half, width),
                b_one,
                b_two,
            )
            for i in range(tiles):
                kept = jnp.where(
                    rank_id < ranks[j, 0, row + i], c[i * half : (i + 1) * half], 0.0
                ).astype(jnp.bfloat16)
                if own:
                    recv[i, slots(m, j, 1)] = kept
                else:
                    send[m, i, pl.ds(j * half, half)] = kept

        for k in range(n - 1):
            m = k + 1
            if leading:
                near = k + n // 2 if k < n // 2 else k - n // 2 + 1
                m = inner * near + (1 - inner) * m
            tile_block(m, False)
            if leading:
                first_copy(m).start()
        tile_block(0, True)

        for o in range(3):
            load_band_wait(o, j)
        c = product(
            vb[:, j, 0].reshape(3 * half, width), vb[:, j, 1].reshape(3 * half, width), b_one, b_two
        ).astype(jnp.bfloat16)
        for o in range(3):
            cband[o, j + o] = c[o * half : (o + 1) * half]

    def load_band_wait(o, j):
        pltpu.make_async_copy(
            v_hbm.at[0, 0, j, :, pl.ds(half, half), :], vb.at[o, j], sem_vb.at[o, j]
        ).wait()

    for block in range(blocks):
        spectra(0, block)
        if block == 0:
            pl.semaphore_wait(barrier, n + nf - 2)
        share_spectra(0, block)
    if tiles > 2:
        for block in range(blocks):
            for q in range(2):
                load_traces(q, 2, block).start()
    for block in range(blocks):
        spectra(1, block)
        share_spectra(1, block)
    if tiles > 3:
        for block in range(blocks):
            for q in range(2):
                load_traces(q, 3, block).start()
    for j in range(2, tiles):
        load_v(j).start()
    coefficients(0, True)
    band_copy(1).start()
    for m in range(n):
        load_u(m).start()
    for j in range(tiles):
        for o in range(3):
            load_band(o, j, False).start()

    def advance(step, _):
        @pl.when(step < tiles)
        def _():
            for block in range(blocks):
                spectra(step, block)
                share_spectra(step, block)

        @pl.when(step + 2 < tiles)
        def _():
            for block in range(blocks):
                for q in range(2):
                    load_traces(q, step + 2, block).start()

        coefficients(step - 1, False)
        return 0

    lax.fori_loop(2, tiles + 1, advance, 0)

    def send_rows(i, _):
        for m in range(1, n):
            row_copy(m, i).start()
        return 0

    band_copy(0).start()
    lax.fori_loop(0, tiles, send_rows, 0)

    for m in range(n):
        load_u(m).wait()
    for j in range(tiles):
        for o in range(3):
            load_band(o, j, False).wait()
    for m in range(1, n):
        first_copy(m).wait_recv()
    band_copy(0).wait_recv()
    band_copy(1).wait_recv()
    zero = jnp.zeros((half, lanes), jnp.bfloat16)
    bin_[0] = jnp.where(first == 0, bin_[0], zero)
    bin_[1] = jnp.where(last == 0, bin_[1], zero)
    cband[2, 0 + 1] = bin_[0]
    cband[0, tiles] = bin_[1]
    gsum[...] = jnp.zeros_like(gsum)

    def transposed(c, u):
        return lax.dot_general(c, u, TN_DIMS, preferred_element_type=jnp.float32)

    def add_source(m, i):
        c = recv[i, slots(m, 0, tiles)]
        for part in range(2):
            u = u_s[i, pl.ds(m * tiles, tiles), part].reshape(tiles * half, width)
            acc[part] += transposed(c, u)

    def respond(i, _):
        c = jnp.concatenate([cband[o, i + 1] for o in range(3)], axis=0)
        for part in range(2):
            acc[part] = transposed(c, ub[:, i, part].reshape(3 * half, width))
        add_source(0, i)

        def from_peer(m, _):
            row_copy(m, i).wait_recv()
            add_source(m, i)
            return 0

        lax.fori_loop(1, n, from_peer, 0)
        parts = []
        for p, (other, sign) in enumerate(((2, -1), (3, 1), (0, 1), (1, -1))):
            one = acc[0, p * count : (p + 1) * count]
            two = acc[1, other * count : (other + 1) * count]
            parts.append((one + two if sign > 0 else one - two).astype(jnp.bfloat16))
        for c in range(2):
            minus[0, c, :, columns(i)] = parts[2 * c]
            plus[0, c, :, columns(i)] = parts[2 * c + 1]
        gsum[...] += lax.dot_general(
            jnp.concatenate(parts, axis=0),
            jnp.concatenate([parts[1], parts[3]], axis=0),
            NT_DIMS,
            preferred_element_type=jnp.float32,
        )
        return 0

    lax.fori_loop(0, tiles, respond, 0)

    receivers = total_tiles * width
    share = count // n
    outs = (cross, normal)
    for q, scale in enumerate((1.0 / math.sqrt(receivers), 1.0 / receivers)):
        top = slice(q * count, (q + 1) * count)
        low = slice((2 + q) * count, (3 + q) * count)
        real = (gsum[top, :count] + gsum[low, count:]) * scale
        imag = (gsum[low, :count] - gsum[top, count:]) * scale
        for d in range(n):
            gsend[d, q, 0] = real[d * share : (d + 1) * share].astype(jnp.bfloat16)
            gsend[d, q, 1] = imag[d * share : (d + 1) * share].astype(jnp.bfloat16)
    for m in range(n - 1, 0, -1):
        gram_copy(m).start()
    for q, scale in enumerate((1.0 / math.sqrt(receivers), 1.0 / receivers)):
        mine = pl.ds(pl.multiple_of(q * count + me * share, share), share)
        under = pl.ds(pl.multiple_of((2 + q) * count + me * share, share), share)
        outs[q][0, 0] = (gsum[mine, :count] + gsum[under, count:]) * scale
        outs[q][0, 1] = (gsum[under, :count] - gsum[mine, count:]) * scale
    for m in range(1, n):
        gram_copy(m).wait_recv()
        for q in range(2):
            outs[q][0] += grecv[m, q].astype(jnp.float32)

    for j in range(tiles):
        for block in range(blocks):
            for g in range(1, nf):
                freq_copy(g, j, block).wait_send()
        for m in range(1, n):
            row_copy(m, j).wait_send()
    for m in range(1, n):
        first_copy(m).wait_send()
    band_copy(0).wait_send()
    band_copy(1).wait_send()
    for m in range(1, n):
        gram_copy(m).wait_send()


def hand_over(count, *refs):
    copies = [
        pltpu.make_async_copy(refs[k], refs[count + k], refs[2 * count].at[k]) for k in range(count)
    ]
    for copy in copies:
        copy.start()
    for copy in copies:
        copy.wait()


def on_device(n, nf, plus_time, minus_time, gate_starts, tile_ranks, u_factors, v_factors):
    freq_total = u_factors.shape[0] * nf
    tiles = v_factors.shape[2]
    half = v_factors.shape[4] // 2
    width = v_factors.shape[5]
    sl, samples, receivers = plus_time.shape
    table = gate_table(freq_total, samples)
    sources = math.gcd(16, sl)
    blocks = sl // sources
    rows = freq_total * 2 * sources
    count = sl * nf
    lanes = 4 * count
    share = count // n
    bf16, f32 = jnp.bfloat16, jnp.float32
    vmem = pl.BlockSpec(memory_space=pltpu.VMEM)
    anywhere = pl.BlockSpec(memory_space=pl.ANY)
    dma = pltpu.SemaphoreType.DMA
    starts = gate_starts.T
    ranks = tile_ranks.transpose(2, 0, 1)
    shapes = (
            jax.ShapeDtypeStruct((1, 2, count, receivers), bf16),
            jax.ShapeDtypeStruct((1, 2, count, receivers), bf16),
            jax.ShapeDtypeStruct((1, 2, share, count), f32),
            jax.ShapeDtypeStruct((1, 2, share, count), f32),
    )
    results = pl.pallas_call(
        functools.partial(operator_kernel, n, nf),
        out_shape=tuple(pltpu.VMEM(shape.shape, shape.dtype) for shape in shapes),
        in_specs=[anywhere] * 7,
        out_specs=(vmem, vmem, vmem, vmem),
        scratch_shapes=[
            pltpu.SMEM(starts.shape, jnp.int32),
            pltpu.SMEM(ranks.shape, jnp.int32),
            pltpu.VMEM(table.shape, f32),
            pltpu.VMEM((rows, 2 * samples), f32),
            pltpu.VMEM((freq_total, 2, 2, sl, receivers), bf16),
            pltpu.VMEM((2, 2, sl, samples, width), bf16),
            pltpu.VMEM((2, 2, count, receivers), bf16),
            pltpu.VMEM((tiles, n * tiles, 2, half, width), bf16),
            pltpu.VMEM((tiles, n * tiles, 2, half, width), bf16),
            pltpu.VMEM((3, tiles, 2, half, width), bf16),
            pltpu.VMEM((3, tiles, 2, half, width), bf16),
            pltpu.VMEM((n, tiles, tiles * half, lanes), bf16),
            pltpu.VMEM((tiles, n * tiles * half, lanes), bf16),
            pltpu.VMEM((3, tiles + 2, half, lanes), bf16),
            pltpu.VMEM((2, half, lanes), bf16),
            pltpu.VMEM((2, lanes, width), f32),
            pltpu.VMEM((lanes, 2 * count), f32),
            pltpu.VMEM((n, 2, 2, share, count), bf16),
            pltpu.VMEM((n, 2, 2, share, count), bf16),
            dma((3,)),
            dma((2, tiles, blocks)),
            dma((tiles,)),
            dma((n,)),
            dma((3, tiles)),
            dma((3, tiles)),
            dma((nf, tiles, blocks)),
            dma((nf, tiles, blocks)),
            dma((n,)),
            dma((n,)),
            dma((n, tiles)),
            dma((n, tiles)),
            dma((2,)),
            dma((2,)),
            dma((n,)),
            dma((n,)),
        ],
        compiler_params=pltpu.CompilerParams(
            collective_id=0, has_side_effects=True, vmem_limit_bytes=57 << 20
        ),
        name="reflection_operator",
    )(starts, ranks, table, plus_time, minus_time, u_factors, v_factors)
    return pl.pallas_call(
        functools.partial(hand_over, len(shapes)),
        out_shape=shapes,
        in_specs=[vmem] * len(shapes),
        out_specs=[anywhere] * len(shapes),
        scratch_shapes=[dma((len(shapes),))],
        compiler_params=pltpu.CompilerParams(vmem_limit_bytes=4 << 20),
        name="hand_over",
    )(*results)


def solution(mesh):
    placed = (
        P("freq", None, "tile"),
        P("freq", None, "tile"),
        P("freq", "tile"),
        P("freq", None, "tile"),
        P("freq", "tile", None, None, None, None),
        P("freq", None, "tile", None, None, None),
    )
    return jax.shard_map(
        functools.partial(on_device, mesh.shape["tile"], mesh.shape["freq"]),
        mesh=mesh,
        in_specs=placed,
        out_specs=(
            P("freq", None, None, "tile"),
            P("freq", None, None, "tile"),
            P("freq", None, "tile", None),
            P("freq", None, "tile", None),
        ),
        check_vma=False,
    )
```

time: 253 us -> 229 us (0.905)
  Pallas kernels: 241 us -> 228 us
  local copies, waits for them, and re-layouts: 10.2 us -> 0.01 us
    pallas_call x1 -> x2, Pallas kernels: 241 us -> 228 us  [the longest x1 227 us: on_device(): pl.pallas_call(functools.partial(operator_kernel, n, nf), out_shape=tuple...]
    unnamed x7 -> x0, local copies, waits for them, and re-layouts: 10.2 us -> none
where the time goes in v1:
time: 229 us
  Pallas kernels  228 us (100%)
    pallas_call x1, Pallas kernels, on_device(): pl.pallas_call(functools.partial(operator_kernel, n, nf), out_shape=tuple...  227 us

profile of v1, /device:TPU:0, one launch (start us, length us, event | category | flops | bytes accessed | tf_op | source)
XLA Modules:
  0.0 229.3 jit_solution(6647973680149053916)
XLA Ops:
  0.6 0.1 multiply_convert_fusion
  0.7 0.6 maximum_convert_fusion.table_hbm
  1.3 226.8 %reflection_operator.1 = (bf16[1,2,128,1536]{3,2,1,0:T(8,128)(2,1)S(1)}, bf16[1,2,128,1536]{3,2,1,0:T(8,128)(2,1)S(1)}, f32[1,2,16,128]{3,2,1,0:T(8,128)S(1)}, f32[1,2,16,128]{3,2,1,0:T(8,128)S(1)}) custom-call(s32[6,32]{1,0:T(8,128)} %bitcast.6, s32[6,1,48]{2,1,0:T(1,128)} %bitcast.7, f32[8,256]{1,0:T(8,128)} %maximum_convert_fusion.table_hbm, ...), custom_call_target="tpu_custom_call" | custom-call | tf_op jit(solution)/shard_map/reflection_operator/pallas_call | solution.py:473
  228.2 1.2 hand_over.1
  (2 shorter events, 0.0 us)

commit v2 on v1

--- a/solution.py
+++ b/solution.py
@@ -3,6 +3,7 @@
 
 import jax
 import jax.numpy as jnp
+import numpy as np
 from jax import lax
 from jax.experimental import pallas as pl
 from jax.experimental.pallas import tpu as pltpu
@@ -14,21 +15,13 @@
 TN_DIMS = (((0,), (0,)), ((), ()))
 
 
-def make_table(freq_count, sample_count):
-    freq_ids = lax.broadcasted_iota(jnp.int32, (freq_count, sample_count), 0)
-    sample_ids = lax.broadcasted_iota(jnp.int32, (freq_count, sample_count), 1)
-    phase_ids = freq_ids * sample_ids % sample_count
-    angles = phase_ids.astype(jnp.float32) * (2.0 * math.pi / sample_count)
-    amplitude = 1.0 / math.sqrt(GATE)
-    return jnp.stack([jnp.cos(angles) * amplitude, -jnp.sin(angles) * amplitude]).astype(
-        jnp.bfloat16
-    )
-
-
-def gate_table(freq_total, samples):
-    table = make_table(freq_total, samples).transpose(1, 0, 2).astype(jnp.float32)
-    table = table.reshape(freq_total * 2, samples)
-    return jnp.concatenate([table, table], axis=1)
+def gate_table(freq_count, sample_count):
+    phase_ids = np.arange(freq_count)[:, None] * np.arange(sample_count)[None] % sample_count
+    angles = phase_ids.astype(np.float32) * np.float32(2.0 * math.pi / sample_count)
+    amplitude = np.float32(1.0 / math.sqrt(GATE))
+    table = np.stack([np.cos(angles) * amplitude, -np.sin(angles) * amplitude], axis=1)
+    table = table.reshape(freq_count * 2, sample_count).astype(jnp.bfloat16).astype(np.float32)
+    return np.concatenate([table, table], axis=1)
 
 
 def partner(me, step, n):
@@ -58,6 +51,10 @@
     sl = spec.shape[3]
     count = sl * nf
     lanes = 4 * count
+    groups = xall.shape[0]
+    near = nf // groups
+    chunk = near * sl
+    group_lanes = 4 * chunk
     base = me * tiles
     total_tiles = n * tiles
     samples = traces.shape[3]
@@ -102,13 +99,15 @@
     def columns(j):
         return pl.ds(pl.multiple_of(j * width, width), width)
 
+    def own_rows(block):
+        return pl.ds(pl.multiple_of(mf % near * sl + block * sources, sources), sources)
+
     def freq_copy(g, j, block):
         peer = partner(mf, g, nf)
         part = pl.ds(block * sources, sources)
-        place = pl.ds(pl.multiple_of(mf * sl + block * sources, sources), sources)
         return pltpu.make_async_remote_copy(
             src_ref=spec.at[peer, :, :, part, columns(j)],
-            dst_ref=xall.at[:, :, place, columns(j)],
+            dst_ref=xall.at[mf // near, :, :, own_rows(block), columns(j)],
             send_sem=fsend.at[g, j, block],
             recv_sem=frecv.at[g, j, block],
             device_id={"freq": peer},
@@ -118,22 +117,23 @@
     def slots(m, j, size):
         return pl.ds((m * tiles + j) * half, size * half)
 
-    def first_copy(m):
+    def first_copy(m, d):
+        h = partner(mf // near, d, groups)
         return pltpu.make_async_remote_copy(
-            src_ref=send.at[m, :, pl.ds(0, half)],
-            dst_ref=recv.at[:, slots(m, 0, 1)],
-            send_sem=csend.at[m],
-            recv_sem=crecv.at[m],
+            src_ref=send.at[h, m, :, pl.ds(0, half)],
+            dst_ref=recv.at[h, :, slots(m, 0, 1)],
+            send_sem=csend.at[m, d],
+            recv_sem=crecv.at[m, d],
             device_id={"tile": partner(me, m, n)},
             device_id_type=MESH,
         )
 
-    def row_copy(m, i):
+    def row_copy(m, i, h):
         return pltpu.make_async_remote_copy(
-            src_ref=send.at[m, i, pl.ds(half, (tiles - 1) * half)],
-            dst_ref=recv.at[i, slots(m, 1, tiles - 1)],
-            send_sem=rsend.at[m, i],
-            recv_sem=rrecv.at[m, i],
+            src_ref=send.at[h, m, i, pl.ds(half, (tiles - 1) * half)],
+            dst_ref=recv.at[h, i, slots(m, 1, tiles - 1)],
+            send_sem=rsend.at[m, i, h],
+            recv_sem=rrecv.at[m, i, h],
             device_id={"tile": partner(me, m, n)},
             device_id_type=MESH,
         )
@@ -204,9 +204,6 @@
     for copy in small_copies:
         copy.wait()
     table[...] = jnp.broadcast_to(small[...][:, None, :], shape).reshape(rows, 2 * samples)
-
-    def own_rows(block):
-        return pl.ds(pl.multiple_of(mf * sl + block * sources, sources), sources)
 
     def spectra(j, block):
         for q in range(2):
@@ -231,53 +228,67 @@
             )
 
     def share_spectra(j, block):
-        for g in range(nf - 1, 0, -1):
+        for g in range(1, nf):
             freq_copy(g, j, block).start()
         part = slice(block * sources, (block + 1) * sources)
-        xall[:, :, own_rows(block), columns(j)] = spec[mf, :, :, part, columns(j)]
-
-    rank_id = lax.broadcasted_iota(jnp.int32, (half, lanes), 0)
+        xall[mf // near, :, :, own_rows(block), columns(j)] = spec[mf, :, :, part, columns(j)]
 
     def product(a_real, a_imag, b_one, b_two):
         return lax.dot_general(
             a_real, b_one, NT_DIMS, preferred_element_type=jnp.float32
         ) + lax.dot_general(a_imag, b_two, NT_DIMS, preferred_element_type=jnp.float32)
 
+    def tile_block(m, j, b_one, b_two, halves, own):
+        row = partner(me, m, n) * tiles
+        rank_id = lax.broadcasted_iota(jnp.int32, (half, b_one.shape[0]), 0)
+        c = product(
+            v_s[j, pl.ds(row, tiles), 0].reshape(tiles * half, width),
+            v_s[j, pl.ds(row, tiles), 1].reshape(tiles * half, width),
+            b_one,
+            b_two,
+        )
+        for i in range(tiles):
+            kept = jnp.where(
+                rank_id < ranks[j, 0, row + i], c[i * half : (i + 1) * half], 0.0
+            ).astype(jnp.bfloat16)
+            for at, h in enumerate(halves):
+                piece = kept[:, at * group_lanes : (at + 1) * group_lanes]
+                if own:
+                    recv[h, i, slots(m, j, 1)] = piece
+                else:
+                    send[h, m, i, pl.ds(j * half, half)] = piece
+
+    def first_coefficients(d):
+        for block in range(blocks):
+            for g in range(max(1, d * near), (d + 1) * near):
+                freq_copy(g, 0, block).wait_recv()
+        h = partner(mf // near, d, groups)
+        b_one = xall[h, :, :, :, columns(0)].reshape(group_lanes, width)
+        b_two = swapped(b_one, chunk, 0)
+        for k in range(n - 1):
+            crossing = k + n // 2 if k < n // 2 else k - n // 2 + 1
+            m = inner * crossing + (1 - inner) * (k + 1)
+            tile_block(m, 0, b_one, b_two, [h], False)
+            first_copy(m, d).start()
+        tile_block(0, 0, b_one, b_two, [h], True)
+
     def coefficients(j, leading):
-        for block in range(blocks):
-            for g in range(1, nf):
-                freq_copy(g, j, block).wait_recv()
-        load_v(j).wait()
-        b_one = xall[:, :, :, columns(j)].reshape(lanes, width)
-        b_two = swapped(b_one, count, 0)
-
-        def tile_block(m, own):
-            row = partner(me, m, n) * tiles
-            c = product(
-                v_s[j, pl.ds(row, tiles), 0].reshape(tiles * half, width),
-                v_s[j, pl.ds(row, tiles), 1].reshape(tiles * half, width),
-                b_one,
-                b_two,
-            )
-            for i in range(tiles):
-                kept = jnp.where(
-                    rank_id < ranks[j, 0, row + i], c[i * half : (i + 1) * half], 0.0
-                ).astype(jnp.bfloat16)
-                if own:
-                    recv[i, slots(m, j, 1)] = kept
-                else:
-                    send[m, i, pl.ds(j * half, half)] = kept
-
-        for k in range(n - 1):
-            m = k + 1
-            if leading:
-                near = k + n // 2 if k < n // 2 else k - n // 2 + 1
-                m = inner * near + (1 - inner) * m
-            tile_block(m, False)
-            if leading:
-                first_copy(m).start()
-        tile_block(0, True)
-
+        if not leading:
+            for block in range(blocks):
+                for g in range(1, nf):
+                    freq_copy(g, j, block).wait_recv()
+            load_v(j).wait()
+        b_one = xall[:, :, :, :, columns(j)].reshape(lanes, width)
+        b_two = jnp.concatenate(
+            [
+                swapped(b_one[h * group_lanes : (h + 1) * group_lanes], chunk, 0)
+                for h in range(groups)
+            ],
+            axis=0,
+        )
+        if not leading:
+            for m in range(n):
+                tile_block(m, j, b_one, b_two, range(groups), m == 0)
         for o in range(3):
             load_band_wait(o, j)
         c = product(
@@ -300,9 +311,13 @@
         for block in range(blocks):
             for q in range(2):
                 load_traces(q, 2, block).start()
+    load_v(0).wait()
+    first_coefficients(0)
     for block in range(blocks):
         spectra(1, block)
         share_spectra(1, block)
+    for d in range(1, groups):
+        first_coefficients(d)
     if tiles > 3:
         for block in range(blocks):
             for q in range(2):
@@ -336,8 +351,9 @@
     lax.fori_loop(2, tiles + 1, advance, 0)
 
     def send_rows(i, _):
-        for m in range(1, n):
-            row_copy(m, i).start()
+        for h in range(groups):
+            for m in range(1, n):
+                row_copy(m, i, h).start()
         return 0
 
     band_copy(0).start()
@@ -349,7 +365,8 @@
         for o in range(3):
             load_band(o, j, False).wait()
     for m in range(1, n):
-        first_copy(m).wait_recv()
+        for d in range(groups):
+            first_copy(m, d).wait_recv()
     band_copy(0).wait_recv()
     band_copy(1).wait_recv()
     zero = jnp.zeros((half, lanes), jnp.bfloat16)
@@ -363,7 +380,7 @@
         return lax.dot_general(c, u, TN_DIMS, preferred_element_type=jnp.float32)
 
     def add_source(m, i):
-        c = recv[i, slots(m, 0, tiles)]
+        c = jnp.concatenate([recv[h, i, slots(m, 0, tiles)] for h in range(groups)], axis=1)
         for part in range(2):
             u = u_s[i, pl.ds(m * tiles, tiles), part].reshape(tiles * half, width)
             acc[part] += transposed(c, u)
@@ -375,16 +392,20 @@
         add_source(0, i)
 
         def from_peer(m, _):
-            row_copy(m, i).wait_recv()
+            for h in range(groups):
+                row_copy(m, i, h).wait_recv()
             add_source(m, i)
             return 0
 
         lax.fori_loop(1, n, from_peer, 0)
         parts = []
         for p, (other, sign) in enumerate(((2, -1), (3, 1), (0, 1), (1, -1))):
-            one = acc[0, p * count : (p + 1) * count]
-            two = acc[1, other * count : (other + 1) * count]
-            parts.append((one + two if sign > 0 else one - two).astype(jnp.bfloat16))
+            blocks_of = []
+            for h in range(groups):
+                one = acc[0, pl.ds(h * group_lanes + p * chunk, chunk)]
+                two = acc[1, pl.ds(h * group_lanes + other * chunk, chunk)]
+                blocks_of.append(one + two if sign > 0 else one - two)
+            parts.append(jnp.concatenate(blocks_of, axis=0).astype(jnp.bfloat16))
         for c in range(2):
             minus[0, c, :, columns(i)] = parts[2 * c]
             plus[0, c, :, columns(i)] = parts[2 * c + 1]
@@ -426,9 +447,11 @@
             for g in range(1, nf):
                 freq_copy(g, j, block).wait_send()
         for m in range(1, n):
-            row_copy(m, j).wait_send()
+            for h in range(groups):
+                row_copy(m, j, h).wait_send()
     for m in range(1, n):
-        first_copy(m).wait_send()
+        for d in range(groups):
+            first_copy(m, d).wait_send()
     band_copy(0).wait_send()
     band_copy(1).wait_send()
     for m in range(1, n):
@@ -458,6 +481,8 @@
     count = sl * nf
     lanes = 4 * count
     share = count // n
+    near = math.gcd(nf, 2)
+    groups = nf // near
     bf16, f32 = jnp.bfloat16, jnp.float32
     vmem = pl.BlockSpec(memory_space=pltpu.VMEM)
     anywhere = pl.BlockSpec(memory_space=pl.ANY)
@@ -482,13 +507,13 @@
             pltpu.VMEM((rows, 2 * samples), f32),
             pltpu.VMEM((freq_total, 2, 2, sl, receivers), bf16),
             pltpu.VMEM((2, 2, sl, samples, width), bf16),
-            pltpu.VMEM((2, 2, count, receivers), bf16),
+            pltpu.VMEM((groups, 2, 2, near * sl, receivers), bf16),
             pltpu.VMEM((tiles, n * tiles, 2, half, width), bf16),
             pltpu.VMEM((tiles, n * tiles, 2, half, width), bf16),
             pltpu.VMEM((3, tiles, 2, half, width), bf16),
             pltpu.VMEM((3, tiles, 2, half, width), bf16),
-            pltpu.VMEM((n, tiles, tiles * half, lanes), bf16),
-            pltpu.VMEM((tiles, n * tiles * half, lanes), bf16),
+            pltpu.VMEM((groups, n, tiles, tiles * half, lanes // groups), bf16),
+            pltpu.VMEM((groups, tiles, n * tiles * half, lanes // groups), bf16),
             pltpu.VMEM((3, tiles + 2, half, lanes), bf16),
             pltpu.VMEM((2, half, lanes), bf16),
             pltpu.VMEM((2, lanes, width), f32),
@@ -503,10 +528,10 @@
             dma((3, tiles)),
             dma((nf, tiles, blocks)),
             dma((nf, tiles, blocks)),
-            dma((n,)),
-            dma((n,)),
-            dma((n, tiles)),
-            dma((n, tiles)),
+            dma((n, groups)),
+            dma((n, groups)),
+            dma((n, tiles, groups)),
+            dma((n, tiles, groups)),
             dma((2,)),
             dma((2,)),
             dma((n,)),

time: 229 us -> 226 us (0.987)
  Pallas kernels: 228 us -> 225 us
    pallas_call x1, Pallas kernels: 227 us -> 224 us  [on_device(): pl.pallas_call(functools.partial(operator_kernel, n, nf), out_shape=tuple...]
where the time goes in v2:
time: 226 us
  Pallas kernels  225 us (100%)
    pallas_call x1, Pallas kernels, on_device(): pl.pallas_call(functools.partial(operator_kernel, n, nf), out_shape=tuple...  224 us

profile of v2, /device:TPU:0, one launch (start us, length us, event | category | flops | bytes accessed | tf_op | source)
XLA Modules:
  0.0 225.9 jit_solution(11820020369529056629)
XLA Ops:
  0.6 224.1 %reflection_operator.1 = (bf16[1,2,128,1536]{3,2,1,0:T(8,128)(2,1)S(1)}, bf16[1,2,128,1536]{3,2,1,0:T(8,128)(2,1)S(1)}, f32[1,2,16,128]{3,2,1,0:T(8,128)S(1)}, f32[1,2,16,128]{3,2,1,0:T(8,128)S(1)}) custom-call(s32[6,32]{1,0:T(8,128)} %bitcast.2, s32[6,1,48]{2,1,0:T(1,128)} %bitcast.3, f32[8,256]{1,0:T(8,128)} %constant.2.clone.table_hbm, ...), custom_call_target="tpu_custom_call" | custom-call | tf_op jit(solution)/shard_map/reflection_operator/pallas_call | solution.py:498
  224.7 1.2 hand_over.1

commit v3 on v2

--- a/solution.py
+++ b/solution.py
@@ -55,6 +55,7 @@
     near = nf // groups
     chunk = near * sl
     group_lanes = 4 * chunk
+    core = mf % near
     base = me * tiles
     total_tiles = n * tiles
     samples = traces.shape[3]
@@ -116,6 +117,9 @@
 
     def slots(m, j, size):
         return pl.ds((m * tiles + j) * half, size * half)
+
+    def across(k):
+        return n // 2 + (1 - core) * k + core * (n // 2 - 1 - k)
 
     def first_copy(m, d):
         h = partner(mf // near, d, groups)
@@ -266,8 +270,9 @@
         b_one = xall[h, :, :, :, columns(0)].reshape(group_lanes, width)
         b_two = swapped(b_one, chunk, 0)
         for k in range(n - 1):
-            crossing = k + n // 2 if k < n // 2 else k - n // 2 + 1
-            m = inner * crossing + (1 - inner) * (k + 1)
+            leading = across(k) if k < n // 2 else k - n // 2 + 1
+            trailing = k + 1 if k < n // 2 - 1 else across(k - n // 2 + 1)
+            m = inner * leading + (1 - inner) * trailing
             tile_block(m, 0, b_one, b_two, [h], False)
             first_copy(m, d).start()
         tile_block(0, 0, b_one, b_two, [h], True)
@@ -352,8 +357,10 @@
 
     def send_rows(i, _):
         for h in range(groups):
-            for m in range(1, n):
+            for m in range(1, n // 2):
                 row_copy(m, i, h).start()
+            for k in range(n // 2):
+                row_copy(across(k), i, h).start()
         return 0
 
     band_copy(0).start()
@@ -397,7 +404,8 @@
             add_source(m, i)
             return 0
 
-        lax.fori_loop(1, n, from_peer, 0)
+        lax.fori_loop(1, n // 2, from_peer, 0)
+        lax.fori_loop(0, n // 2, lambda k, _: from_peer(across(k), _), 0)
         parts = []
         for p, (other, sign) in enumerate(((2, -1), (3, 1), (0, 1), (1, -1))):
             blocks_of = []

time: 226 us -> 223 us (0.987)
  Pallas kernels: 225 us -> 222 us
    pallas_call x1, Pallas kernels: 224 us -> 221 us  [on_device(): pl.pallas_call(functools.partial(operator_kernel, n, nf), out_shape=tuple...]
where the time goes in v3:
time: 223 us
  Pallas kernels  222 us (100%)
    pallas_call x1, Pallas kernels, on_device(): pl.pallas_call(functools.partial(operator_kernel, n, nf), out_shape=tuple...  221 us

profile of v3, /device:TPU:0, one launch (start us, length us, event | category | flops | bytes accessed | tf_op | source)
XLA Modules:
  0.0 223.0 jit_solution(6417184327151566370)
XLA Ops:
  0.6 221.2 %reflection_operator.1 = (bf16[1,2,128,1536]{3,2,1,0:T(8,128)(2,1)S(1)}, bf16[1,2,128,1536]{3,2,1,0:T(8,128)(2,1)S(1)}, f32[1,2,16,128]{3,2,1,0:T(8,128)S(1)}, f32[1,2,16,128]{3,2,1,0:T(8,128)S(1)}) custom-call(s32[6,32]{1,0:T(8,128)} %bitcast.2, s32[6,1,48]{2,1,0:T(1,128)} %bitcast.3, f32[8,256]{1,0:T(8,128)} %constant.2.clone.table_hbm, ...), custom_call_target="tpu_custom_call" | custom-call | tf_op jit(solution)/shard_map/reflection_operator/pallas_call | solution.py:506
  221.8 1.2 hand_over.1
